TPU v7x, 32 devices: a whole 2x2x4 slice. The times are simulated.
32 devices in a mesh: row: 4 (over x, core), col: 8 (over z, y).
Axes of the slice: x: 2, y: 2, z: 4, core: 2. Of those that a mesh axis runs over, the one named last changes fastest.
Arguments:
- matrix: float32 [2048, 2048], P('row', 'col'), as said below
- panel: float32 [2048, 256], P(('row', 'col')), may hold values from -0.125 to 0.125
- factor: float32 [256, 256], replicated, as said below
Outputs:
- updated: float32 [2048, 2048], P('row', 'col')
- correction: float32 [2048, 256], P(('row', 'col'))
Inputs may be any that keep to these rules, and one draw needn't show every extreme that they name: `matrix`: symmetric. `factor`: upper triangular with a positive diagonal.
All inputs are finite; a program needn't handle non-finite values.
Results may differ from a plain program's by a relative error of at most 0.000071.
Values sent between devices are 32-bit elements; how exact they have to be, the bound alone decides.
A program may use at most 64 MiB of HBM per device.

v0:
```python
import jax
import jax.numpy as jnp
from jax import lax
from jax.sharding import PartitionSpec as P


def from_root(value, axis, source):
    kept = jnp.where(lax.axis_index(axis) == source, value, 0).astype(value.dtype)
    return lax.psum(kept, axis)


def mult(left, right):
    return jnp.dot(left, right, precision=lax.Precision.HIGHEST, preferred_element_type=jnp.float32)


def per_device(matrix, panel, factor):
    ncols = lax.axis_size("col")
    nrows = lax.axis_size("row")
    blocks = panel.shape[0]
    col_index = lax.axis_index("col")
    col_rows = blocks * nrows
    offset = col_index * nrows % ncols * blocks
    owner = col_index * nrows // ncols
    row_panel = lax.all_gather(panel, "col", axis=0, tiled=True)
    col_panel = from_root(lax.dynamic_slice_in_dim(row_panel, offset, col_rows, 0), "row", owner)
    product = lax.psum(mult(matrix, col_panel), "col")
    scaled = mult(product, factor)
    small = lax.psum(mult(row_panel.T, scaled), "row")
    row_corr = scaled - 0.5 * mult(row_panel, mult(factor.T, small))
    correction = lax.dynamic_slice_in_dim(row_corr, col_index * blocks, blocks, 0)
    col_corr = from_root(lax.dynamic_slice_in_dim(row_corr, offset, col_rows, 0), "row", owner)
    updated = matrix - mult(row_panel, col_corr.T) - mult(row_corr, col_panel.T)
    return (updated, correction)


def solution(mesh):
    in_specs = (P("row", "col"), P(("row", "col"), None), P())
    out_specs = (P("row", "col"), P(("row", "col"), None))
    return jax.shard_map(
        per_device, mesh=mesh, in_specs=in_specs, out_specs=out_specs, check_vma=False
    )
```

profile of v0, /device:TPU:0, one launch (start us, length us, event | category | flops | bytes accessed | tf_op | source)
XLA Modules:
  0.0 231.1 jit_solution(12882593466567161444)
XLA Ops:
  7.2 0.0 copy-start
  7.2 0.0 all-reduce.5.cloned.1.call-start
  7.2 33.2 %all_gather.3 = f32[512,256]{1,0:T(8,128)S(1)} all-gather(f32[64,256]{1,0:T(8,128)} %param.4), channel_id=1, replica_groups=mesh['row'=4,'col'=8] {'col'}, dimensions={0}, use_global_device_ids=true | all-gather | bytes 589824 | tf_op jit(solution)/shard_map/all_gather | solution.py:24
  40.5 0.0 copy-start.1
  40.5 0.7 dynamic-slice_select_fusion.1
  41.2 0.0 all-reduce.5.cloned.1.call-update
  41.2 0.0 all-reduce.7.cloned.1.call-start
  41.3 33.5 %all-reduce.5.cloned.1.call-done = f32[256,256]{1,0:T(8,128)} async-done(((f32[256,256]{1,0:T(8,128)}), f32[256,256]{1,0:T(8,128)}) %all-reduce.5.cloned.1.call-update) | async-done | bytes 262160 | tf_op jit(solution)/shard_map/psum | solution.py:9
  74.8 0.0 copy-done.1
  74.8 2.8 %convolution_bitcast_fusion.1 = f32[512,256]{0,1:T(8,128)} fusion(f32[256,256]{1,0:T(8,128)} %all-reduce.5.cloned.1.call-done, f32[512,256]{1,0:T(8,128)S(1)} %copy-done.1), kind=kOutput, calls=%fused_computation.1 | convolution fusion | flops 402653184 | bytes 1310720 | tf_op jit(solution)/shard_map/dot_general | solution.py:13
  77.6 0.0 all-reduce.7.cloned.1.call-update
  77.6 0.0 all-reduce.9.cloned.1.call-start
  77.6 73.8 %all-reduce.7.cloned.1.call-done = f32[512,256]{0,1:T(8,128)} async-done(((f32[512,256]{0,1:T(8,128)}), f32[512,256]{0,1:T(8,128)}) %all-reduce.7.cloned.1.call-update) | async-done | bytes 524304 | tf_op jit(solution)/shard_map/psum | solution.py:26
  151.5 0.0 copy-done
  151.5 2.0 fusion.4
  153.5 1.7 convolution_bitcast_fusion.2
  155.2 0.0 all-reduce.9.cloned.1.call-update
  155.3 0.0 all-reduce.11.cloned.1.call-start
  155.3 0.2 copy.6
  155.5 31.4 %all-reduce.9.cloned.1.call-done = f32[256,256]{0,1:T(8,128)} async-done(((f32[256,256]{0,1:T(8,128)}), f32[256,256]{0,1:T(8,128)}) %all-reduce.9.cloned.1.call-update) | async-done | bytes 262160 | tf_op jit(solution)/shard_map/psum | solution.py:28
  186.9 1.3 fusion.5
  188.2 0.6 fusion.3
  188.8 0.7 dynamic-slice_select_fusion
  189.5 0.0 copy-start.2
  189.6 0.0 all-reduce.11.cloned.1.call-update
  189.6 0.9 copy-done.2
  190.5 0.6 fusion.6
  191.1 0.6 constant_dynamic-slice_fusion
  191.8 30.2 %all-reduce.11.cloned.1.call-done = f32[256,256]{1,0:T(8,128)} async-done(((f32[256,256]{1,0:T(8,128)}), f32[256,256]{1,0:T(8,128)}) %all-reduce.11.cloned.1.call-update) | async-done | bytes 262160 | tf_op jit(solution)/shard_map/psum | solution.py:9
  222.0 1.6 fusion.1
  223.6 1.0 copy.8
Async XLA Ops:
  7.2 144.3 %copy-start = (f32[256,256]{1,0:T(8,128)S(1)}, f32[256,256]{1,0:T(8,128)}, u32[]{:S(2)}) copy-start(f32[256,256]{1,0:T(8,128)} %param.5) | copy-start | bytes 786436
  7.2 67.6 %all-reduce.5.cloned.1.call-start = ((), (), s32[]{:S(2)}) async-start(), calls=%async_computation | async-start | bytes 524288 | tf_op jit(solution)/shard_map/psum | solution.py:9
  40.5 34.3 %copy-start.1 = (f32[512,256]{1,0:T(8,128)S(1)}, f32[512,256]{1,0:T(8,128)}, u32[]{:S(2)}) copy-start(f32[512,256]{1,0:T(8,128)} %param.3) | copy-start | bytes 1572868
  41.2 110.2 %all-reduce.7.cloned.1.call-start = ((), (), s32[]{:S(2)}) async-start(), calls=%async_computation.1 | async-start | bytes 1048576 | tf_op jit(solution)/shard_map/psum | solution.py:26
  77.6 109.3 %all-reduce.9.cloned.1.call-start = ((), (), s32[]{:S(2)}) async-start(), calls=%async_computation.2 | async-start | bytes 524288 | tf_op jit(solution)/shard_map/psum | solution.py:28
  155.3 66.8 %all-reduce.11.cloned.1.call-start = ((), (), s32[]{:S(2)}) async-start(), calls=%async_computation.3 | async-start | bytes 524288 | tf_op jit(solution)/shard_map/psum | solution.py:9
  189.5 0.9 copy-start.2
Sparse Core Ops, SparseCore 0:
  41.4 33.3 all-reduce.4
  78.8 72.6 all-reduce.6
  155.4 31.4 all-reduce.8
  189.7 32.2 all-reduce.10
where the time goes:
time: 231 us
  waiting for transfers between devices  169 us (73%)
  blocking collectives  33.2 us (14%)
  between operations  13.8 us (6%)
  matrix products  10.7 us (5%)
  local copies, waits for them, and re-layouts  2.77 us (1%)
    psum x1, waiting for transfers between devices, per_device(): product = lax.psum(mult(matrix, col_panel), 'col')  73.8 us
    psum x2, waiting for transfers between devices, from_root(): return lax.psum(kept, axis)  63.7 us
    all_gather x1, blocking collectives, per_device(): row_panel = lax.all_gather(panel, 'col', axis=0, tiled=True)  33.2 us
    psum x1, waiting for transfers between devices, per_device(): small = lax.psum(mult(row_panel.T, scaled), 'row')  31.4 us
    dot_general x7, matrix products, mult(): jnp.dot(left, right, precision=lax.Precision.HIGHEST, preferred_element_t...  10.7 us
  transfers between devices with their start and end apart: 4, of which 4 were waited for; matrix products, arithmetic and copies ran while one was open for 1% of the time, Pallas kernels for 0%

commit v1 on v0

v1 whole, which is shorter than its diff:
```python
import functools

import jax
import jax.numpy as jnp
from jax import lax
from jax.experimental import pallas as pl
from jax.experimental.pallas import tpu as pltpu
from jax.sharding import PartitionSpec as P

F32 = jnp.float32
BF16 = jnp.bfloat16
NN = (((1,), (0,)), ((), ()))
NT = (((1,), (1,)), ((), ()))


def split(x):
    high = x.astype(BF16)
    return high, (x - high.astype(F32)).astype(BF16)


def mult(a, b, dims=NN):
    dot = functools.partial(lax.dot_general, dimension_numbers=dims, preferred_element_type=F32)
    return dot(a[0], b[1]) + dot(a[1], b[0]) + dot(a[0], b[0])


def tile_loop(count, body):
    if count <= 2:
        for i in range(count):
            body(i)
    else:
        pl.loop(0, count)(body)


def kernel(nrows, ncols, tile, a_ref, panel_ref, t_ref, out_ref, corr_ref,
           vr, vc, sr, sc, q, qin, kpart, kin, kfull, at_hi, at_lo, vt_hi, vt_lo,
           v_send, v_recv, vf_send, vf_recv, q_send, q_recv, sc_send, sc_recv,
           s_send, s_recv, sf_send, sf_recv, vc_send, vc_recv, k_send, k_recv, kg_send, kg_recv):
    r, c = lax.axis_index("row"), lax.axis_index("col")
    lines = ncols // 2
    group = ncols // (2 * nrows)
    z, y = c // 2, c % 2
    blk, width = panel_ref.shape
    total = a_ref.shape[0]
    tiles = total // tile
    kblk = width // nrows
    ndev = nrows * ncols
    me = r * ncols + c

    def rows(index, size):
        return pl.ds(pl.multiple_of(index * size, size), size)

    def copy(src, dst, send, recv, row, col):
        return pltpu.make_async_remote_copy(
            src_ref=src, dst_ref=dst, send_sem=send, recv_sem=recv,
            device_id=(row, col), device_id_type=pl.DeviceIdType.MESH)

    barrier = pltpu.get_barrier_semaphore()

    @pl.loop(1, ndev)
    def _(d):
        other = lax.rem(me + d, ndev)
        pl.semaphore_signal(barrier, inc=1, device_id=(other // ncols, lax.rem(other, ncols)),
                            device_id_type=pl.DeviceIdType.MESH)

    vr[rows(c, blk), :] = panel_ref[...]
    pl.semaphore_wait(barrier, ndev - 1)
    sends = []

    def go(desc):
        desc.start()
        sends.append(desc)

    for d in range(1, lines):
        go(copy(panel_ref, vr.at[rows(c, blk)], v_send.at[d], v_recv.at[d], r, lax.rem(z + d, lines) * 2 + y))
    go(copy(panel_ref, vr.at[rows(c, blk)], v_send.at[0], v_recv.at[0], r, z * 2 + 1 - y))

    def flip(i):
        lo_i = pl.ds(pl.multiple_of(i * tile, tile), tile)
        high, low = split(a_ref[lo_i, :].T)
        at_hi[i] = high
        at_lo[i] = low
    tile_loop(tiles, flip)
    t_two = split(t_ref[...])

    for d in range(1, lines):
        source = lax.rem(z - d + lines, lines) * 2 + y
        slot = vr.at[rows(source, blk)]
        copy(panel_ref, slot, v_send.at[d], v_recv.at[d], r, c).wait_recv()
        go(copy(slot, slot, vf_send.at[d], vf_recv.at[d], r, z * 2 + 1 - y))
    copy(panel_ref, vr.at[rows(z * 2 + 1 - y, blk)], v_send.at[0], v_recv.at[0], r, c).wait_recv()
    for d in range(1, lines):
        source = lax.rem(z - d + lines, lines) * 2 + 1 - y
        slot = vr.at[rows(source, blk)]
        copy(slot, slot, vf_send.at[d], vf_recv.at[d], r, c).wait_recv()

    q[...] = jnp.zeros_like(q)

    def gather_product(i):
        q[...] += mult((at_hi[i], at_lo[i]), split(vr[pl.ds(pl.multiple_of(i * tile, tile), tile), :]))
    tile_loop(tiles, gather_product)

    for d in range(1, nrows):
        other = lax.rem(r + d, nrows)
        go(copy(q.at[rows(other, blk)], qin.at[d], q_send.at[d], q_recv.at[d], other, c))

    def turn(i):
        high, low = split(mult(split(vr[pl.ds(pl.multiple_of(i * tile, tile), tile), :]), t_two).T)
        vt_hi[i] = high
        vt_lo[i] = low
    tile_loop(tiles, turn)

    for d in range(1, nrows):
        copy(qin.at[d], qin.at[d], q_send.at[d], q_recv.at[d], r, c).wait_recv()
    product = q[rows(r, blk), :]
    for d in range(1, nrows):
        product = product + qin[d]
    mine = sc.at[rows(r, blk)]
    sc[rows(r, blk), :] = mult(split(product), t_two)

    for d in range(1, nrows):
        go(copy(mine, mine, sc_send.at[d], sc_recv.at[d], lax.rem(r + d, nrows), c))
    target = z // group
    local = lax.rem(c * nrows + r, ncols)
    here = r * group + lax.rem(z, group)
    for d in range(1, lines):
        go(copy(mine, sr.at[rows(local, blk)], s_send.at[d], s_recv.at[here], target,
                lax.rem(z + d, lines) * 2 + y))

    holder = c * nrows // ncols
    v_slice = vr.at[rows(lax.rem(c * nrows, ncols) // nrows, nrows * blk)]

    @pl.when(r == holder)
    def _():
        for d in range(1, nrows):
            copy(v_slice, vc, vc_send.at[d], vc_recv.at[0], lax.rem(r + d, nrows), c).start()
        vc[...] = v_slice[...]

    for d in range(1, nrows):
        slot = sc.at[rows(lax.rem(r - d + nrows, nrows), blk)]
        copy(slot, slot, sc_send.at[d], sc_recv.at[d], r, c).wait_recv()

    for g in range(group):
        line = r * group + g
        for j in range(nrows):
            place = lax.rem((line * 2 + y) * nrows + j, ncols)
            slot = sr.at[rows(place, blk)]

            @pl.when(z == line)
            def _():
                slot[...] = sc[j * blk:(j + 1) * blk, :]

            @pl.when(z != line)
            def _():
                copy(slot, slot, s_send.at[1], s_recv.at[j * group + g], r, c).wait_recv()

            go(copy(slot, slot, sf_send.at[j * group + g], sf_recv.at[j * group + g], r, z * 2 + 1 - y))
    for g in range(group):
        line = r * group + g
        for j in range(nrows):
            place = lax.rem((line * 2 + 1 - y) * nrows + j, ncols)
            slot = sr.at[rows(place, blk)]
            copy(slot, slot, sf_send.at[j * group + g], sf_recv.at[j * group + g], r, c).wait_recv()

    kpart[...] = jnp.zeros_like(kpart)

    def inner(i):
        kpart[...] += mult((vt_hi[i], vt_lo[i]), split(sr[pl.ds(pl.multiple_of(i * tile, tile), tile), :]))
    tile_loop(tiles, inner)

    for d in range(1, nrows):
        other = lax.rem(r + d, nrows)
        go(copy(kpart.at[rows(other, kblk)], kin.at[d], k_send.at[d], k_recv.at[d], other, c))

    @pl.when(r != holder)
    def _():
        copy(vc, vc, vc_send.at[1], vc_recv.at[0], r, c).wait_recv()

    for d in range(1, nrows):
        copy(kin.at[d], kin.at[d], k_send.at[d], k_recv.at[d], r, c).wait_recv()
    summed = kpart[rows(r, kblk), :]
    for d in range(1, nrows):
        summed = summed + kin[d]
    kmine = kfull.at[rows(r, kblk)]
    kfull[rows(r, kblk), :] = summed
    for d in range(1, nrows):
        go(copy(kmine, kmine, kg_send.at[d], kg_recv.at[d], lax.rem(r + d, nrows), c))

    vc_two = split(vc[...])

    def first(i):
        span = pl.ds(pl.multiple_of(i * tile, tile), tile)
        out_ref[span, :] = a_ref[span, :] - mult(split(sr[span, :]), vc_two, NT)
    tile_loop(tiles, first)

    for d in range(1, nrows):
        slot = kfull.at[rows(lax.rem(r - d + nrows, nrows), kblk)]
        copy(slot, slot, kg_send.at[d], kg_recv.at[d], r, c).wait_recv()

    k_two = split(kfull[...])
    y_two = split(sc[...] - mult(vc_two, k_two))

    def second(i):
        span = pl.ds(pl.multiple_of(i * tile, tile), tile)
        out_ref[span, :] = out_ref[span, :] - mult(split(vr[span, :]), y_two, NT)
    tile_loop(tiles, second)
    corr_ref[...] = sr[rows(c, blk), :] - 0.5 * mult(split(panel_ref[...]), k_two)

    for desc in sends:
        desc.wait_send()

    @pl.when(r == holder)
    def _():
        for d in range(1, nrows):
            copy(v_slice, vc, vc_send.at[d], vc_recv.at[0], r, c).wait_send()


def per_device(nrows, ncols, matrix, panel, factor):
    total, wide = matrix.shape
    blk, width = panel.shape
    tile = min(256, total)
    tiles = total // tile
    group = ncols // (2 * nrows)
    lines = ncols // 2
    dma = pltpu.SemaphoreType.DMA
    vmem = pl.BlockSpec(memory_space=pltpu.VMEM)
    return pl.pallas_call(
        functools.partial(kernel, nrows, ncols, tile),
        out_shape=(jax.ShapeDtypeStruct(matrix.shape, F32), jax.ShapeDtypeStruct(panel.shape, F32)),
        in_specs=[vmem] * 3,
        out_specs=(vmem, vmem),
        scratch_shapes=[
            pltpu.VMEM((total, width), F32),
            pltpu.VMEM((wide, width), F32),
            pltpu.VMEM((total, width), F32),
            pltpu.VMEM((wide, width), F32),
            pltpu.VMEM((wide, width), F32),
            pltpu.VMEM((nrows, blk, width), F32),
            pltpu.VMEM((width, width), F32),
            pltpu.VMEM((nrows, width // nrows, width), F32),
            pltpu.VMEM((width, width), F32),
            pltpu.VMEM((tiles, wide, tile), BF16),
            pltpu.VMEM((tiles, wide, tile), BF16),
            pltpu.VMEM((tiles, width, tile), BF16),
            pltpu.VMEM((tiles, width, tile), BF16),
            dma((lines,)), dma((lines,)), dma((lines,)), dma((lines,)),
            dma((nrows,)), dma((nrows,)), dma((nrows,)), dma((nrows,)),
            dma((lines,)), dma((nrows * group,)), dma((nrows * group,)), dma((nrows * group,)),
            dma((nrows,)), dma((1,)), dma((nrows,)), dma((nrows,)), dma((nrows,)), dma((nrows,)),
        ],
        compiler_params=pltpu.CompilerParams(
            collective_id=0, has_side_effects=True, vmem_limit_bytes=60 * 1024 * 1024),
    )(matrix, panel, factor)


def solution(mesh):
    in_specs = (P("row", "col"), P(("row", "col"), None), P())
    out_specs = (P("row", "col"), P(("row", "col"), None))
    return jax.shard_map(
        functools.partial(per_device, mesh.shape["row"], mesh.shape["col"]),
        mesh=mesh, in_specs=in_specs, out_specs=out_specs, check_vma=False)
```

time: 231 us -> 50.2 us (0.22)
  waiting for transfers between devices: 169 us -> 0 us
  Pallas kernels: 0 us -> 46.2 us
  blocking collectives: 33.2 us -> 0 us
  between operations: 13.8 us -> 0.65 us
  matrix products: 10.7 us -> 0 us
    psum x4 -> x0, waiting for transfers between devices: 169 us -> none  [the longest x1 73.8 us: per_device(): product = lax.psum(mult(matrix, col_panel), 'col')]
    pallas_call x0 -> x1, Pallas kernels: none -> 46.2 us  [per_device(): pl.pallas_call(functools.partial(kernel, nrows, ncols, tile), out_shape=(...]
    all_gather x1 -> x0, blocking collectives: 33.2 us -> none  [per_device(): row_panel = lax.all_gather(panel, 'col', axis=0, tiled=True)]
    dot_general x7 -> x0, matrix products: 10.7 us -> none  [mult(): jnp.dot(left, right, precision=lax.Precision.HIGHEST, preferred_element_t...]
  transfers between devices with their start and end apart: 4 -> 0, of which waited for: 4 -> 0; matrix products, arithmetic and copies ran while one was open for 1% -> 0% of each run, Pallas kernels for 0% -> 0%
where the time goes in v1:
time: 50.2 us; the launch traced here: 49.4 us
  Pallas kernels  46.2 us (92%)
  local copies, waits for them, and re-layouts  2.53 us (5%)
  between operations  0.65 us (1%)
    pallas_call x1, Pallas kernels, per_device(): pl.pallas_call(functools.partial(kernel, nrows, ncols, tile), out_shape=(...  46.2 us
    unnamed x4, local copies, waits for them, and re-layouts  2.53 us

profile of v1, /device:TPU:0, one launch (start us, length us, event | category | flops | bytes accessed | tf_op | source)
XLA Modules:
  0.0 49.4 jit_solution(10253782315863299246)
XLA Ops:
  0.6 46.2 %shard_map.50 = (f32[512,256]{1,0:T(8,128)}, f32[64,256]{1,0:T(8,128)}) custom-call(f32[512,256]{1,0:T(8,128)} %a_ref.1, f32[64,256]{1,0:T(8,128)} %panel_ref.1, f32[256,256]{1,0:T(8,128)} %t_ref.1), custom_call_target="tpu_custom_call" | custom-call | tf_op jit(solution)/shard_map/pallas_call | solution.py:226
  46.9 0.0 copy-start
  46.9 1.9 %copy.7 = f32[512,256]{1,0:T(8,128)} copy(f32[512,256]{1,0:T(8,128)} %get-tuple-element.4) | data formatting | bytes 1048576
  48.8 0.0 copy-done
  48.8 0.6 %copy.8 = f32[64,256]{1,0:T(8,128)} copy(f32[64,256]{1,0:T(8,128)S(1)} %copy-done) | data formatting | bytes 131072
Async XLA Ops:
  46.9 1.9 %copy-start = (f32[64,256]{1,0:T(8,128)S(1)}, f32[64,256]{1,0:T(8,128)}, u32[]{:S(2)}) copy-start(f32[64,256]{1,0:T(8,128)} %get-tuple-element.5) | copy-start | bytes 196612

commit v2 on v1

--- a/solution.py
+++ b/solution.py
@@ -32,7 +32,7 @@
 
 
 def kernel(nrows, ncols, tile, a_ref, panel_ref, t_ref, out_ref, corr_ref,
-           vr, vc, sr, sc, q, qin, kpart, kin, kfull, at_hi, at_lo, vt_hi, vt_lo,
+           vr, vc, sr, sc, q, qin, kpart, kin, kpair, kfull, at_hi, at_lo, vt_hi, vt_lo,
            v_send, v_recv, vf_send, vf_recv, q_send, q_recv, sc_send, sc_recv,
            s_send, s_recv, sf_send, sf_recv, vc_send, vc_recv, k_send, k_recv, kg_send, kg_recv):
     r, c = lax.axis_index("row"), lax.axis_index("col")
@@ -42,9 +42,8 @@
     blk, width = panel_ref.shape
     total = a_ref.shape[0]
     tiles = total // tile
-    kblk = width // nrows
-    ndev = nrows * ncols
-    me = r * ncols + c
+    half = width // 2
+    mate = r + 1 - 2 * (r % 2)
 
     def rows(index, size):
         return pl.ds(pl.multiple_of(index * size, size), size)
@@ -56,15 +55,36 @@
 
     barrier = pltpu.get_barrier_semaphore()
 
-    @pl.loop(1, ndev)
-    def _(d):
-        other = lax.rem(me + d, ndev)
-        pl.semaphore_signal(barrier, inc=1, device_id=(other // ncols, lax.rem(other, ncols)),
-                            device_id_type=pl.DeviceIdType.MESH)
+    def greet(row, col):
+        pl.semaphore_signal(barrier, inc=1, device_id=(row, col), device_id_type=pl.DeviceIdType.MESH)
+
+    target = z // group
+    for d in range(1, lines):
+        greet(r, lax.rem(z + d, lines) * 2 + y)
+    greet(r, z * 2 + 1 - y)
+    for d in range(1, nrows):
+        greet(lax.rem(r + d, nrows), c)
+    for g in range(group):
+        line = r * group + g
+
+        @pl.when(z != line)
+        def _():
+            for d in range(1, nrows):
+                greet(lax.rem(r + d, nrows), line * 2 + y)
 
     vr[rows(c, blk), :] = panel_ref[...]
-    pl.semaphore_wait(barrier, ndev - 1)
+    pl.semaphore_wait(barrier, lines + nrows - 1 + jnp.where(target == r, 0, lines - 1))
     sends = []
+    vc_sent = []
+
+    def finish():
+        for desc in sends:
+            desc.wait_send()
+        if vc_sent:
+            @pl.when(r == holder)
+            def _():
+                for d in range(1, nrows):
+                    copy(v_slice, vc, vc_send.at[d], vc_recv.at[0], lax.rem(r + d, nrows), c).wait_send()
 
     def go(desc):
         desc.start()
@@ -119,7 +139,6 @@
 
     for d in range(1, nrows):
         go(copy(mine, mine, sc_send.at[d], sc_recv.at[d], lax.rem(r + d, nrows), c))
-    target = z // group
     local = lax.rem(c * nrows + r, ncols)
     here = r * group + lax.rem(z, group)
     for d in range(1, lines):
@@ -128,6 +147,8 @@
 
     holder = c * nrows // ncols
     v_slice = vr.at[rows(lax.rem(c * nrows, ncols) // nrows, nrows * blk)]
+
+    vc_sent.append(True)
 
     @pl.when(r == holder)
     def _():
@@ -167,23 +188,16 @@
         kpart[...] += mult((vt_hi[i], vt_lo[i]), split(sr[pl.ds(pl.multiple_of(i * tile, tile), tile), :]))
     tile_loop(tiles, inner)
 
-    for d in range(1, nrows):
-        other = lax.rem(r + d, nrows)
-        go(copy(kpart.at[rows(other, kblk)], kin.at[d], k_send.at[d], k_recv.at[d], other, c))
+    go(copy(kpart.at[rows(mate % 2, half)], kin.at[0], k_send.at[0], k_recv.at[0], mate, c))
 
     @pl.when(r != holder)
     def _():
         copy(vc, vc, vc_send.at[1], vc_recv.at[0], r, c).wait_recv()
 
-    for d in range(1, nrows):
-        copy(kin.at[d], kin.at[d], k_send.at[d], k_recv.at[d], r, c).wait_recv()
-    summed = kpart[rows(r, kblk), :]
-    for d in range(1, nrows):
-        summed = summed + kin[d]
-    kmine = kfull.at[rows(r, kblk)]
-    kfull[rows(r, kblk), :] = summed
-    for d in range(1, nrows):
-        go(copy(kmine, kmine, kg_send.at[d], kg_recv.at[d], lax.rem(r + d, nrows), c))
+    copy(kin.at[0], kin.at[0], k_send.at[0], k_recv.at[0], r, c).wait_recv()
+    kpair[...] = kpart[rows(r % 2, half), :] + kin[0]
+    for d in range(1, nrows // 2):
+        go(copy(kpair, kin.at[d], k_send.at[d], k_recv.at[d], lax.rem(r + 2 * d, nrows), c))
 
     vc_two = split(vc[...])
 
@@ -192,9 +206,16 @@
         out_ref[span, :] = a_ref[span, :] - mult(split(sr[span, :]), vc_two, NT)
     tile_loop(tiles, first)
 
-    for d in range(1, nrows):
-        slot = kfull.at[rows(lax.rem(r - d + nrows, nrows), kblk)]
-        copy(slot, slot, kg_send.at[d], kg_recv.at[d], r, c).wait_recv()
+    for d in range(1, nrows // 2):
+        copy(kpair, kin.at[d], k_send.at[d], k_recv.at[d], r, c).wait_recv()
+    summed = kpair[...]
+    for d in range(1, nrows // 2):
+        summed = summed + kin[d]
+    mine_half = kfull.at[rows(r % 2, half)]
+    mine_half[...] = summed
+    go(copy(mine_half, mine_half, kg_send.at[0], kg_recv.at[0], mate, c))
+    other_half = kfull.at[rows(mate % 2, half)]
+    copy(other_half, other_half, kg_send.at[0], kg_recv.at[0], r, c).wait_recv()
 
     k_two = split(kfull[...])
     y_two = split(sc[...] - mult(vc_two, k_two))
@@ -205,13 +226,7 @@
     tile_loop(tiles, second)
     corr_ref[...] = sr[rows(c, blk), :] - 0.5 * mult(split(panel_ref[...]), k_two)
 
-    for desc in sends:
-        desc.wait_send()
-
-    @pl.when(r == holder)
-    def _():
-        for d in range(1, nrows):
-            copy(v_slice, vc, vc_send.at[d], vc_recv.at[0], r, c).wait_send()
+    finish()
 
 
 def per_device(nrows, ncols, matrix, panel, factor):
@@ -236,7 +251,8 @@
             pltpu.VMEM((wide, width), F32),
             pltpu.VMEM((nrows, blk, width), F32),
             pltpu.VMEM((width, width), F32),
-            pltpu.VMEM((nrows, width // nrows, width), F32),
+            pltpu.VMEM((nrows // 2, width // 2, width), F32),
+            pltpu.VMEM((width // 2, width), F32),
             pltpu.VMEM((width, width), F32),
             pltpu.VMEM((tiles, wide, tile), BF16),
             pltpu.VMEM((tiles, wide, tile), BF16),

time: 50.2 us -> 49.3 us (0.982); the launches traced: 49.4 us -> 49.1 us
  no operation moved by 1% of the time
where the time goes in v2:
time: 49.3 us; the launch traced here: 49.1 us
  Pallas kernels  45.9 us (93%)
  local copies, waits for them, and re-layouts  2.53 us (5%)
  between operations  0.65 us (1%)
    pallas_call x1, Pallas kernels, per_device(): pl.pallas_call(functools.partial(kernel, nrows, ncols, tile), out_shape=(...  45.9 us
    unnamed x4, local copies, waits for them, and re-layouts  2.53 us

profile of v2, /device:TPU:0, one launch (start us, length us, event | category | flops | bytes accessed | tf_op | source)
XLA Modules:
  0.0 49.1 jit_solution(8882208352457261496)
XLA Ops:
  0.6 45.9 %shard_map.50 = (f32[512,256]{1,0:T(8,128)}, f32[64,256]{1,0:T(8,128)}) custom-call(f32[512,256]{1,0:T(8,128)} %a_ref.1, f32[64,256]{1,0:T(8,128)} %panel_ref.1, f32[256,256]{1,0:T(8,128)} %t_ref.1), custom_call_target="tpu_custom_call" | custom-call | tf_op jit(solution)/shard_map/pallas_call | solution.py:241
  46.6 0.0 copy-start
  46.6 1.9 %copy.7 = f32[512,256]{1,0:T(8,128)} copy(f32[512,256]{1,0:T(8,128)} %get-tuple-element.4) | data formatting | bytes 1048576
  48.5 0.0 copy-done
  48.5 0.6 %copy.8 = f32[64,256]{1,0:T(8,128)} copy(f32[64,256]{1,0:T(8,128)S(1)} %copy-done) | data formatting | bytes 131072
Async XLA Ops:
  46.6 1.9 %copy-start = (f32[64,256]{1,0:T(8,128)S(1)}, f32[64,256]{1,0:T(8,128)}, u32[]{:S(2)}) copy-start(f32[64,256]{1,0:T(8,128)} %get-tuple-element.5) | copy-start | bytes 196612

commit v3 on v2

--- a/solution.py
+++ b/solution.py
@@ -75,24 +75,55 @@
     vr[rows(c, blk), :] = panel_ref[...]
     pl.semaphore_wait(barrier, lines + nrows - 1 + jnp.where(target == r, 0, lines - 1))
     sends = []
-    vc_sent = []
+    holder = c * nrows // ncols
+    first_block = lax.rem(c * nrows, ncols)
+    near = sorted((o for o in range(1 - lines, lines) if o), key=abs)
+
+    def each_line(offsets, body):
+        for o in offsets:
+            line = z + o
+            pl.when((line >= 0) & (line < lines))(functools.partial(body, line))
 
     def finish():
         for desc in sends:
             desc.wait_send()
-        if vc_sent:
-            @pl.when(r == holder)
-            def _():
-                for d in range(1, nrows):
-                    copy(v_slice, vc, vc_send.at[d], vc_recv.at[0], lax.rem(r + d, nrows), c).wait_send()
+        for d in range(lines):
+            line = lax.rem(z + d, lines)
+            copy(panel_ref, panel_ref, v_send.at[line], v_recv.at[line], r, c).wait_send()
+            if d:
+                copy(panel_ref, panel_ref, vf_send.at[line], vf_recv.at[line], r, c).wait_send()
+                copy(panel_ref, panel_ref, s_send.at[line], s_recv.at[0], r, c).wait_send()
+
+        for i in range(nrows * group):
+            copy(panel_ref, panel_ref, sf_send.at[i], sf_recv.at[i], r, c).wait_send()
+
+        @pl.when(r == holder)
+        def _():
+            for d in range(1, nrows):
+                for j in range(nrows):
+                    copy(panel_ref, panel_ref, vc_send.at[d, j], vc_recv.at[j], r, c).wait_send()
 
     def go(desc):
         desc.start()
         sends.append(desc)
 
-    for d in range(1, lines):
-        go(copy(panel_ref, vr.at[rows(c, blk)], v_send.at[d], v_recv.at[d], r, lax.rem(z + d, lines) * 2 + y))
-    go(copy(panel_ref, vr.at[rows(c, blk)], v_send.at[0], v_recv.at[0], r, z * 2 + 1 - y))
+    def pass_on(src, column):
+        j = column - first_block
+
+        @pl.when((r == holder) & (j >= 0) & (j < nrows))
+        def _():
+            for d in range(1, nrows):
+                copy(src, vc.at[rows(j, blk)], vc_send.at[d, j], vc_recv.at[j],
+                     lax.rem(r + d, nrows), c).start()
+
+    across = z * 2 + 1 - y
+    own = vr.at[rows(c, blk)]
+    copy(panel_ref, own, v_send.at[z], v_recv.at[z], r, across).start()
+
+    def send_panel(line):
+        copy(panel_ref, own, v_send.at[line], v_recv.at[z], r, line * 2 + y).start()
+    each_line(near, send_panel)
+    pass_on(panel_ref, c)
 
     def flip(i):
         lo_i = pl.ds(pl.multiple_of(i * tile, tile), tile)
@@ -102,16 +133,23 @@
     tile_loop(tiles, flip)
     t_two = split(t_ref[...])
 
-    for d in range(1, lines):
-        source = lax.rem(z - d + lines, lines) * 2 + y
-        slot = vr.at[rows(source, blk)]
-        copy(panel_ref, slot, v_send.at[d], v_recv.at[d], r, c).wait_recv()
-        go(copy(slot, slot, vf_send.at[d], vf_recv.at[d], r, z * 2 + 1 - y))
-    copy(panel_ref, vr.at[rows(z * 2 + 1 - y, blk)], v_send.at[0], v_recv.at[0], r, c).wait_recv()
-    for d in range(1, lines):
-        source = lax.rem(z - d + lines, lines) * 2 + 1 - y
-        slot = vr.at[rows(source, blk)]
-        copy(slot, slot, vf_send.at[d], vf_recv.at[d], r, c).wait_recv()
+    def forward(line):
+        slot = vr.at[rows(line * 2 + y, blk)]
+        copy(slot, slot, v_send.at[line], v_recv.at[line], r, c).wait_recv()
+        copy(slot, slot, vf_send.at[line], vf_recv.at[line], r, across).start()
+        pass_on(slot, line * 2 + y)
+
+    def arrive(line):
+        slot = vr.at[rows(line * 2 + 1 - y, blk)]
+        copy(slot, slot, vf_send.at[line], vf_recv.at[line], r, c).wait_recv()
+        pass_on(slot, line * 2 + 1 - y)
+
+    each_line(near[:2], forward)
+    slot = vr.at[rows(across, blk)]
+    copy(slot, slot, v_send.at[z], v_recv.at[z], r, c).wait_recv()
+    pass_on(slot, across)
+    each_line(near[2:], forward)
+    each_line(near, arrive)
 
     q[...] = jnp.zeros_like(q)
 
@@ -137,24 +175,18 @@
     mine = sc.at[rows(r, blk)]
     sc[rows(r, blk), :] = mult(split(product), t_two)
 
-    for d in range(1, nrows):
-        go(copy(mine, mine, sc_send.at[d], sc_recv.at[d], lax.rem(r + d, nrows), c))
     local = lax.rem(c * nrows + r, ncols)
     here = r * group + lax.rem(z, group)
-    for d in range(1, lines):
-        go(copy(mine, sr.at[rows(local, blk)], s_send.at[d], s_recv.at[here], target,
-                lax.rem(z + d, lines) * 2 + y))
-
-    holder = c * nrows // ncols
-    v_slice = vr.at[rows(lax.rem(c * nrows, ncols) // nrows, nrows * blk)]
-
-    vc_sent.append(True)
+
+    def send_scaled(line):
+        copy(mine, sr.at[rows(local, blk)], s_send.at[line], s_recv.at[here], target, line * 2 + y).start()
+    each_line(near[::-1], send_scaled)
+    for d in range(1, nrows):
+        go(copy(mine, mine, sc_send.at[d], sc_recv.at[d], lax.rem(r + d, nrows), c))
 
     @pl.when(r == holder)
     def _():
-        for d in range(1, nrows):
-            copy(v_slice, vc, vc_send.at[d], vc_recv.at[0], lax.rem(r + d, nrows), c).start()
-        vc[...] = v_slice[...]
+        vc[...] = vr[rows(first_block // nrows, nrows * blk), :]
 
     for d in range(1, nrows):
         slot = sc.at[rows(lax.rem(r - d + nrows, nrows), blk)]
@@ -162,19 +194,21 @@
 
     for g in range(group):
         line = r * group + g
-        for j in range(nrows):
+        for d in range(nrows):
+            j = lax.rem(r + d, nrows)
             place = lax.rem((line * 2 + y) * nrows + j, ncols)
             slot = sr.at[rows(place, blk)]
 
             @pl.when(z == line)
             def _():
-                slot[...] = sc[j * blk:(j + 1) * blk, :]
+                held = sc.at[rows(j, blk)]
+                copy(held, slot, sf_send.at[j * group + g], sf_recv.at[j * group + g], r, across).start()
+                slot[...] = held[...]
 
             @pl.when(z != line)
             def _():
-                copy(slot, slot, s_send.at[1], s_recv.at[j * group + g], r, c).wait_recv()
-
-            go(copy(slot, slot, sf_send.at[j * group + g], sf_recv.at[j * group + g], r, z * 2 + 1 - y))
+                copy(slot, slot, s_send.at[0], s_recv.at[j * group + g], r, c).wait_recv()
+                copy(slot, slot, sf_send.at[j * group + g], sf_recv.at[j * group + g], r, across).start()
     for g in range(group):
         line = r * group + g
         for j in range(nrows):
@@ -192,7 +226,8 @@
 
     @pl.when(r != holder)
     def _():
-        copy(vc, vc, vc_send.at[1], vc_recv.at[0], r, c).wait_recv()
+        for j in range(nrows):
+            copy(panel_ref, panel_ref, vc_send.at[1, j], vc_recv.at[j], r, c).wait_recv()
 
     copy(kin.at[0], kin.at[0], k_send.at[0], k_recv.at[0], r, c).wait_recv()
     kpair[...] = kpart[rows(r % 2, half), :] + kin[0]
@@ -261,7 +296,7 @@
             dma((lines,)), dma((lines,)), dma((lines,)), dma((lines,)),
             dma((nrows,)), dma((nrows,)), dma((nrows,)), dma((nrows,)),
             dma((lines,)), dma((nrows * group,)), dma((nrows * group,)), dma((nrows * group,)),
-            dma((nrows,)), dma((1,)), dma((nrows,)), dma((nrows,)), dma((nrows,)), dma((nrows,)),
+            dma((nrows, nrows)), dma((nrows,)), dma((nrows,)), dma((nrows,)), dma((nrows,)), dma((nrows,)),
         ],
         compiler_params=pltpu.CompilerParams(
             collective_id=0, has_side_effects=True, vmem_limit_bytes=60 * 1024 * 1024),

time: 49.3 us -> 52.6 us (1.067); the launches traced: 49.1 us -> 51.9 us
  Pallas kernels: 45.9 us -> 48.7 us
    pallas_call x1, Pallas kernels: 45.9 us -> 48.7 us  [per_device(): pl.pallas_call(functools.partial(kernel, nrows, ncols, tile), out_shape=(...]
where the time goes in v3:
time: 52.6 us; the launch traced here: 51.9 us
  Pallas kernels  48.7 us (93%)
  local copies, waits for them, and re-layouts  2.53 us (5%)
  between operations  0.65 us (1%)
    pallas_call x1, Pallas kernels, per_device(): pl.pallas_call(functools.partial(kernel, nrows, ncols, tile), out_shape=(...  48.7 us
    unnamed x4, local copies, waits for them, and re-layouts  2.53 us

profile of v3, /device:TPU:0, one launch (start us, length us, event | category | flops | bytes accessed | tf_op | source)
XLA Modules:
  0.0 51.9 jit_solution(5905604223897598150)
XLA Ops:
  0.6 48.7 %shard_map.50 = (f32[512,256]{1,0:T(8,128)}, f32[64,256]{1,0:T(8,128)}) custom-call(f32[512,256]{1,0:T(8,128)} %a_ref.1, f32[64,256]{1,0:T(8,128)} %panel_ref.1, f32[256,256]{1,0:T(8,128)} %t_ref.1), custom_call_target="tpu_custom_call" | custom-call | tf_op jit(solution)/shard_map/pallas_call | solution.py:276
  49.3 0.0 copy-start
  49.3 1.9 %copy.7 = f32[512,256]{1,0:T(8,128)} copy(f32[512,256]{1,0:T(8,128)} %get-tuple-element.4) | data formatting | bytes 1048576
  51.2 0.0 copy-done
  51.2 0.6 %copy.8 = f32[64,256]{1,0:T(8,128)} copy(f32[64,256]{1,0:T(8,128)S(1)} %copy-done) | data formatting | bytes 131072
Async XLA Ops:
  49.3 1.9 %copy-start = (f32[64,256]{1,0:T(8,128)S(1)}, f32[64,256]{1,0:T(8,128)}, u32[]{:S(2)}) copy-start(f32[64,256]{1,0:T(8,128)} %get-tuple-element.5) | copy-start | bytes 196612

commit v4 on v3

--- a/solution.py
+++ b/solution.py
@@ -97,25 +97,19 @@
         for i in range(nrows * group):
             copy(panel_ref, panel_ref, sf_send.at[i], sf_recv.at[i], r, c).wait_send()
 
+        @pl.when(r % 2 == holder % 2)
+        def _():
+            copy(vc, vc, vc_send.at[0], vc_recv.at[0], r, c).wait_send()
+
         @pl.when(r == holder)
         def _():
-            for d in range(1, nrows):
-                for j in range(nrows):
-                    copy(panel_ref, panel_ref, vc_send.at[d, j], vc_recv.at[j], r, c).wait_send()
+            for d in range(1, nrows // 2):
+                copy(vc, vc, vc_send.at[d], vc_recv.at[0], r, c).wait_send()
 
     def go(desc):
         desc.start()
         sends.append(desc)
 
-    def pass_on(src, column):
-        j = column - first_block
-
-        @pl.when((r == holder) & (j >= 0) & (j < nrows))
-        def _():
-            for d in range(1, nrows):
-                copy(src, vc.at[rows(j, blk)], vc_send.at[d, j], vc_recv.at[j],
-                     lax.rem(r + d, nrows), c).start()
-
     across = z * 2 + 1 - y
     own = vr.at[rows(c, blk)]
     copy(panel_ref, own, v_send.at[z], v_recv.at[z], r, across).start()
@@ -123,7 +117,6 @@
     def send_panel(line):
         copy(panel_ref, own, v_send.at[line], v_recv.at[z], r, line * 2 + y).start()
     each_line(near, send_panel)
-    pass_on(panel_ref, c)
 
     def flip(i):
         lo_i = pl.ds(pl.multiple_of(i * tile, tile), tile)
@@ -137,17 +130,14 @@
         slot = vr.at[rows(line * 2 + y, blk)]
         copy(slot, slot, v_send.at[line], v_recv.at[line], r, c).wait_recv()
         copy(slot, slot, vf_send.at[line], vf_recv.at[line], r, across).start()
-        pass_on(slot, line * 2 + y)
 
     def arrive(line):
         slot = vr.at[rows(line * 2 + 1 - y, blk)]
         copy(slot, slot, vf_send.at[line], vf_recv.at[line], r, c).wait_recv()
-        pass_on(slot, line * 2 + 1 - y)
 
     each_line(near[:2], forward)
     slot = vr.at[rows(across, blk)]
     copy(slot, slot, v_send.at[z], v_recv.at[z], r, c).wait_recv()
-    pass_on(slot, across)
     each_line(near[2:], forward)
     each_line(near, arrive)
 
@@ -183,10 +173,6 @@
     each_line(near[::-1], send_scaled)
     for d in range(1, nrows):
         go(copy(mine, mine, sc_send.at[d], sc_recv.at[d], lax.rem(r + d, nrows), c))
-
-    @pl.when(r == holder)
-    def _():
-        vc[...] = vr[rows(first_block // nrows, nrows * blk), :]
 
     for d in range(1, nrows):
         slot = sc.at[rows(lax.rem(r - d + nrows, nrows), blk)]
@@ -209,6 +195,14 @@
             def _():
                 copy(slot, slot, s_send.at[0], s_recv.at[j * group + g], r, c).wait_recv()
                 copy(slot, slot, sf_send.at[j * group + g], sf_recv.at[j * group + g], r, across).start()
+    @pl.when(r == holder)
+    def _():
+        v_slice = vr.at[rows(first_block // nrows, nrows * blk)]
+        for d in range(1, nrows // 2):
+            copy(v_slice, vc, vc_send.at[d], vc_recv.at[0], lax.rem(r + 2 * d, nrows), c).start()
+        copy(v_slice, vc, vc_send.at[0], vc_recv.at[0], mate, c).start()
+        vc[...] = v_slice[...]
+
     for g in range(group):
         line = r * group + g
         for j in range(nrows):
@@ -226,8 +220,11 @@
 
     @pl.when(r != holder)
     def _():
-        for j in range(nrows):
-            copy(panel_ref, panel_ref, vc_send.at[1, j], vc_recv.at[j], r, c).wait_recv()
+        copy(vc, vc, vc_send.at[0], vc_recv.at[0], r, c).wait_recv()
+
+    @pl.when((r != holder) & (r % 2 == holder % 2))
+    def _():
+        copy(vc, vc, vc_send.at[0], vc_recv.at[0], mate, c).start()
 
     copy(kin.at[0], kin.at[0], k_send.at[0], k_recv.at[0], r, c).wait_recv()
     kpair[...] = kpart[rows(r % 2, half), :] + kin[0]
@@ -296,7 +293,7 @@
             dma((lines,)), dma((lines,)), dma((lines,)), dma((lines,)),
             dma((nrows,)), dma((nrows,)), dma((nrows,)), dma((nrows,)),
             dma((lines,)), dma((nrows * group,)), dma((nrows * group,)), dma((nrows * group,)),
-            dma((nrows, nrows)), dma((nrows,)), dma((nrows,)), dma((nrows,)), dma((nrows,)), dma((nrows,)),
+            dma((nrows,)), dma((1,)), dma((nrows,)), dma((nrows,)), dma((nrows,)), dma((nrows,)),
         ],
         compiler_params=pltpu.CompilerParams(
             collective_id=0, has_side_effects=True, vmem_limit_bytes=60 * 1024 * 1024),

time: 52.6 us -> 48.7 us (0.926); the launches traced: 51.9 us -> 48.5 us
  Pallas kernels: 48.7 us -> 45.3 us
    pallas_call x1, Pallas kernels: 48.7 us -> 45.3 us  [per_device(): pl.pallas_call(functools.partial(kernel, nrows, ncols, tile), out_shape=(...]
where the time goes in v4:
time: 48.7 us; the launch traced here: 48.5 us
  Pallas kernels  45.3 us (93%)
  local copies, waits for them, and re-layouts  2.53 us (5%)
  between operations  0.65 us (1%)
    pallas_call x1, Pallas kernels, per_device(): pl.pallas_call(functools.partial(kernel, nrows, ncols, tile), out_shape=(...  45.3 us
    unnamed x4, local copies, waits for them, and re-layouts  2.53 us

profile of v4, /device:TPU:0, one launch (start us, length us, event | category | flops | bytes accessed | tf_op | source)
XLA Modules:
  0.0 48.5 jit_solution(11211383647605995201)
XLA Ops:
  0.6 45.3 %shard_map.50 = (f32[512,256]{1,0:T(8,128)}, f32[64,256]{1,0:T(8,128)}) custom-call(f32[512,256]{1,0:T(8,128)} %a_ref.1, f32[64,256]{1,0:T(8,128)} %panel_ref.1, f32[256,256]{1,0:T(8,128)} %t_ref.1), custom_call_target="tpu_custom_call" | custom-call | tf_op jit(solution)/shard_map/pallas_call | solution.py:273
  46.0 0.0 copy-start
  46.0 1.9 %copy.7 = f32[512,256]{1,0:T(8,128)} copy(f32[512,256]{1,0:T(8,128)} %get-tuple-element.4) | data formatting | bytes 1048576
  47.9 0.0 copy-done
  47.9 0.6 %copy.8 = f32[64,256]{1,0:T(8,128)} copy(f32[64,256]{1,0:T(8,128)S(1)} %copy-done) | data formatting | bytes 131072
Async XLA Ops:
  46.0 1.9 %copy-start = (f32[64,256]{1,0:T(8,128)S(1)}, f32[64,256]{1,0:T(8,128)}, u32[]{:S(2)}) copy-start(f32[64,256]{1,0:T(8,128)} %get-tuple-element.5) | copy-start | bytes 196612

commit v5 on v4

--- a/solution.py
+++ b/solution.py
@@ -261,6 +261,11 @@
     finish()
 
 
+def hand_out(held_ref, held_corr_ref, out_ref, corr_ref):
+    out_ref[...] = held_ref[...]
+    corr_ref[...] = held_corr_ref[...]
+
+
 def per_device(nrows, ncols, matrix, panel, factor):
     total, wide = matrix.shape
     blk, width = panel.shape
@@ -270,7 +275,8 @@
     lines = ncols // 2
     dma = pltpu.SemaphoreType.DMA
     vmem = pl.BlockSpec(memory_space=pltpu.VMEM)
-    return pl.pallas_call(
+    limit = 4 * (5 * total * wide + 4 * total * width + 4 * wide * width + 16 * width * width) + (4 << 20)
+    held = pl.pallas_call(
         functools.partial(kernel, nrows, ncols, tile),
         out_shape=(jax.ShapeDtypeStruct(matrix.shape, F32), jax.ShapeDtypeStruct(panel.shape, F32)),
         in_specs=[vmem] * 3,
@@ -296,8 +302,15 @@
             dma((nrows,)), dma((1,)), dma((nrows,)), dma((nrows,)), dma((nrows,)), dma((nrows,)),
         ],
         compiler_params=pltpu.CompilerParams(
-            collective_id=0, has_side_effects=True, vmem_limit_bytes=60 * 1024 * 1024),
+            collective_id=0, has_side_effects=True, vmem_limit_bytes=limit),
     )(matrix, panel, factor)
+    return pl.pallas_call(
+        hand_out,
+        out_shape=(jax.ShapeDtypeStruct(matrix.shape, F32), jax.ShapeDtypeStruct(panel.shape, F32)),
+        in_specs=[vmem] * 2,
+        out_specs=(vmem, vmem),
+        compiler_params=pltpu.CompilerParams(vmem_limit_bytes=6 * total * wide * 4 + (1 << 20)),
+    )(*held)
 
 
 def solution(mesh):

time: 48.7 us -> 47.9 us (0.984)
  Pallas kernels: 45.3 us -> 44.2 us
    pallas_call x1, Pallas kernels: 45.3 us -> 43.4 us  [per_device(): pl.pallas_call(functools.partial(kernel, nrows, ncols, tile), out_shape=(...]
    pallas_call x0 -> x1, Pallas kernels: none -> 0.84 us  [per_device(): pl.pallas_call(hand_out, out_shape=(jax.ShapeDtypeStruct(matrix.shape, F3...]
    unnamed x4 -> x6, local copies, waits for them, and re-layouts: 2.53 us -> 2.82 us
where the time goes in v5:
time: 47.9 us; the launch traced here: 47.7 us
  Pallas kernels  44.2 us (92%)
  local copies, waits for them, and re-layouts  2.82 us (6%)
  between operations  0.65 us (1%)
    pallas_call x1, Pallas kernels, per_device(): pl.pallas_call(functools.partial(kernel, nrows, ncols, tile), out_shape=(...  43.4 us
    unnamed x6, local copies, waits for them, and re-layouts  2.82 us

profile of v5, /device:TPU:0, one launch (start us, length us, event | category | flops | bytes accessed | tf_op | source)
XLA Modules:
  0.0 47.7 jit_solution(428558170893534056)
XLA Ops:
  0.6 0.0 copy-start
  0.6 1.0 %copy-done = f32[512,256]{1,0:T(8,128)S(1)} copy-done((f32[512,256]{1,0:T(8,128)S(1)}, f32[512,256]{1,0:T(8,128)}, u32[]{:S(2)}) %copy-start) | copy-done | bytes 524312
  1.7 0.0 copy-start.1
  1.7 0.9 %copy-done.1 = f32[256,256]{1,0:T(8,128)S(1)} copy-done((f32[256,256]{1,0:T(8,128)S(1)}, f32[256,256]{1,0:T(8,128)}, u32[]{:S(2)}) %copy-start.1) | copy-done | bytes 262168
  2.6 0.0 copy-start.2
  2.6 0.8 %copy-done.2 = f32[64,256]{1,0:T(8,128)S(1)} copy-done((f32[64,256]{1,0:T(8,128)S(1)}, f32[64,256]{1,0:T(8,128)}, u32[]{:S(2)}) %copy-start.2) | copy-done | bytes 65560
  3.5 43.4 %shard_map.50 = (f32[512,256]{1,0:T(8,128)S(1)}, f32[64,256]{1,0:T(8,128)S(1)}) custom-call(f32[512,256]{1,0:T(8,128)S(1)} %copy-done, f32[64,256]{1,0:T(8,128)S(1)} %copy-done.2, f32[256,256]{1,0:T(8,128)S(1)} %copy-done.1), custom_call_target="tpu_custom_call" | custom-call | tf_op jit(solution)/shard_map/pallas_call | solution.py:279
  46.8 0.8 %shard_map.51 = (f32[512,256]{1,0:T(8,128)}, f32[64,256]{1,0:T(8,128)}) custom-call(f32[512,256]{1,0:T(8,128)S(1)} %get-tuple-element.4.held_ref, f32[64,256]{1,0:T(8,128)S(1)} %get-tuple-element.5.held_corr_ref), custom_call_target="tpu_custom_call" | custom-call | tf_op jit(solution)/shard_map/pallas_call | solution.py:307
Async XLA Ops:
  0.6 1.0 %copy-start = (f32[512,256]{1,0:T(8,128)S(1)}, f32[512,256]{1,0:T(8,128)}, u32[]{:S(2)}) copy-start(f32[512,256]{1,0:T(8,128)} %a_ref.1) | copy-start | bytes 1572868
  1.7 0.9 %copy-start.1 = (f32[256,256]{1,0:T(8,128)S(1)}, f32[256,256]{1,0:T(8,128)}, u32[]{:S(2)}) copy-start(f32[256,256]{1,0:T(8,128)} %t_ref.1) | copy-start | bytes 786436
  2.6 0.8 %copy-start.2 = (f32[64,256]{1,0:T(8,128)S(1)}, f32[64,256]{1,0:T(8,128)}, u32[]{:S(2)}) copy-start(f32[64,256]{1,0:T(8,128)} %panel_ref.1) | copy-start | bytes 196612

commit v6 on v5

--- a/solution.py
+++ b/solution.py
@@ -77,12 +77,10 @@
     sends = []
     holder = c * nrows // ncols
     first_block = lax.rem(c * nrows, ncols)
-    near = sorted((o for o in range(1 - lines, lines) if o), key=abs)
-
-    def each_line(offsets, body):
-        for o in offsets:
-            line = z + o
-            pl.when((line >= 0) & (line < lines))(functools.partial(body, line))
+
+    def each_line(body, sign):
+        for d in range(1, lines):
+            body(lax.rem(z + sign * d + lines, lines))
 
     def finish():
         for desc in sends:
@@ -116,7 +114,7 @@
 
     def send_panel(line):
         copy(panel_ref, own, v_send.at[line], v_recv.at[z], r, line * 2 + y).start()
-    each_line(near, send_panel)
+    each_line(send_panel, 1)
 
     def flip(i):
         lo_i = pl.ds(pl.multiple_of(i * tile, tile), tile)
@@ -135,11 +133,10 @@
         slot = vr.at[rows(line * 2 + 1 - y, blk)]
         copy(slot, slot, vf_send.at[line], vf_recv.at[line], r, c).wait_recv()
 
-    each_line(near[:2], forward)
+    each_line(forward, -1)
     slot = vr.at[rows(across, blk)]
     copy(slot, slot, v_send.at[z], v_recv.at[z], r, c).wait_recv()
-    each_line(near[2:], forward)
-    each_line(near, arrive)
+    each_line(arrive, -1)
 
     q[...] = jnp.zeros_like(q)
 
@@ -170,7 +167,7 @@
 
     def send_scaled(line):
         copy(mine, sr.at[rows(local, blk)], s_send.at[line], s_recv.at[here], target, line * 2 + y).start()
-    each_line(near[::-1], send_scaled)
+    each_line(send_scaled, 1)
     for d in range(1, nrows):
         go(copy(mine, mine, sc_send.at[d], sc_recv.at[d], lax.rem(r + d, nrows), c))
 

time: 47.9 us -> 47.6 us (level)
  Pallas kernels: 44.2 us -> 43.6 us
    pallas_call x1, Pallas kernels: 43.4 us -> 42.8 us  [per_device(): pl.pallas_call(functools.partial(kernel, nrows, ncols, tile), out_shape=(...]
where the time goes in v6:
time: 47.6 us; the launch traced here: 47.1 us
  Pallas kernels  43.6 us (92%)
  local copies, waits for them, and re-layouts  2.82 us (6%)
  between operations  0.65 us (1%)
    pallas_call x1, Pallas kernels, per_device(): pl.pallas_call(functools.partial(kernel, nrows, ncols, tile), out_shape=(...  42.8 us
    unnamed x6, local copies, waits for them, and re-layouts  2.82 us

profile of v6, /device:TPU:0, one launch (start us, length us, event | category | flops | bytes accessed | tf_op | source)
XLA Modules:
  0.0 47.1 jit_solution(10880405122347030645)
XLA Ops:
  0.6 0.0 copy-start
  0.6 1.0 %copy-done = f32[512,256]{1,0:T(8,128)S(1)} copy-done((f32[512,256]{1,0:T(8,128)S(1)}, f32[512,256]{1,0:T(8,128)}, u32[]{:S(2)}) %copy-start) | copy-done | bytes 524312
  1.7 0.0 copy-start.1
  1.7 0.9 %copy-done.1 = f32[256,256]{1,0:T(8,128)S(1)} copy-done((f32[256,256]{1,0:T(8,128)S(1)}, f32[256,256]{1,0:T(8,128)}, u32[]{:S(2)}) %copy-start.1) | copy-done | bytes 262168
  2.6 0.0 copy-start.2
  2.6 0.8 %copy-done.2 = f32[64,256]{1,0:T(8,128)S(1)} copy-done((f32[64,256]{1,0:T(8,128)S(1)}, f32[64,256]{1,0:T(8,128)}, u32[]{:S(2)}) %copy-start.2) | copy-done | bytes 65560
  3.5 42.8 %shard_map.50 = (f32[512,256]{1,0:T(8,128)S(1)}, f32[64,256]{1,0:T(8,128)S(1)}) custom-call(f32[512,256]{1,0:T(8,128)S(1)} %copy-done, f32[64,256]{1,0:T(8,128)S(1)} %copy-done.2, f32[256,256]{1,0:T(8,128)S(1)} %copy-done.1), custom_call_target="tpu_custom_call" | custom-call | tf_op jit(solution)/shard_map/pallas_call | solution.py:276
  46.3 0.8 %shard_map.51 = (f32[512,256]{1,0:T(8,128)}, f32[64,256]{1,0:T(8,128)}) custom-call(f32[512,256]{1,0:T(8,128)S(1)} %get-tuple-element.4.held_ref, f32[64,256]{1,0:T(8,128)S(1)} %get-tuple-element.5.held_corr_ref), custom_call_target="tpu_custom_call" | custom-call | tf_op jit(solution)/shard_map/pallas_call | solution.py:304
Async XLA Ops:
  0.6 1.0 %copy-start = (f32[512,256]{1,0:T(8,128)S(1)}, f32[512,256]{1,0:T(8,128)}, u32[]{:S(2)}) copy-start(f32[512,256]{1,0:T(8,128)} %a_ref.1) | copy-start | bytes 1572868
  1.7 0.9 %copy-start.1 = (f32[256,256]{1,0:T(8,128)S(1)}, f32[256,256]{1,0:T(8,128)}, u32[]{:S(2)}) copy-start(f32[256,256]{1,0:T(8,128)} %t_ref.1) | copy-start | bytes 786436
  2.6 0.8 %copy-start.2 = (f32[64,256]{1,0:T(8,128)S(1)}, f32[64,256]{1,0:T(8,128)}, u32[]{:S(2)}) copy-start(f32[64,256]{1,0:T(8,128)} %panel_ref.1) | copy-start | bytes 196612

commit v7 on v6

--- a/solution.py
+++ b/solution.py
@@ -62,6 +62,8 @@
     for d in range(1, lines):
         greet(r, lax.rem(z + d, lines) * 2 + y)
     greet(r, z * 2 + 1 - y)
+    opposite = lax.rem(z + lines // 2, lines)
+    greet(r, opposite * 2 + 1 - y)
     for d in range(1, nrows):
         greet(lax.rem(r + d, nrows), c)
     for g in range(group):
@@ -73,13 +75,15 @@
                 greet(lax.rem(r + d, nrows), line * 2 + y)
 
     vr[rows(c, blk), :] = panel_ref[...]
-    pl.semaphore_wait(barrier, lines + nrows - 1 + jnp.where(target == r, 0, lines - 1))
+    pl.semaphore_wait(barrier, lines + nrows + jnp.where(target == r, 0, lines - 1))
     sends = []
     holder = c * nrows // ncols
     first_block = lax.rem(c * nrows, ncols)
 
-    def each_line(body, sign):
+    def each_line(body, sign, skip=0):
         for d in range(1, lines):
+            if d == skip:
+                continue
             body(lax.rem(z + sign * d + lines, lines))
 
     def finish():
@@ -115,6 +119,7 @@
     def send_panel(line):
         copy(panel_ref, own, v_send.at[line], v_recv.at[z], r, line * 2 + y).start()
     each_line(send_panel, 1)
+    copy(panel_ref, own, vf_send.at[opposite], vf_recv.at[z], r, opposite * 2 + 1 - y).start()
 
     def flip(i):
         lo_i = pl.ds(pl.multiple_of(i * tile, tile), tile)
@@ -133,7 +138,9 @@
         slot = vr.at[rows(line * 2 + 1 - y, blk)]
         copy(slot, slot, vf_send.at[line], vf_recv.at[line], r, c).wait_recv()
 
-    each_line(forward, -1)
+    each_line(forward, -1, lines // 2)
+    slot = vr.at[rows(opposite * 2 + y, blk)]
+    copy(slot, slot, v_send.at[opposite], v_recv.at[opposite], r, c).wait_recv()
     slot = vr.at[rows(across, blk)]
     copy(slot, slot, v_send.at[z], v_recv.at[z], r, c).wait_recv()
     each_line(arrive, -1)

time: 47.6 us -> 47.6 us (level)
  no operation moved by 1% of the time
where the time goes in v7:
time: 47.6 us; the launch traced here: 47 us
  Pallas kernels  43.5 us (91%)
  local copies, waits for them, and re-layouts  2.82 us (6%)
  between operations  0.65 us (1%)
    pallas_call x1, Pallas kernels, per_device(): pl.pallas_call(functools.partial(kernel, nrows, ncols, tile), out_shape=(...  42.7 us
    unnamed x6, local copies, waits for them, and re-layouts  2.82 us

profile of v7, /device:TPU:0, one launch (start us, length us, event | category | flops | bytes accessed | tf_op | source)
XLA Modules:
  0.0 47.0 jit_solution(15765128918739029024)
XLA Ops:
  0.6 0.0 copy-start
  0.6 1.0 %copy-done = f32[512,256]{1,0:T(8,128)S(1)} copy-done((f32[512,256]{1,0:T(8,128)S(1)}, f32[512,256]{1,0:T(8,128)}, u32[]{:S(2)}) %copy-start) | copy-done | bytes 524312
  1.7 0.0 copy-start.1
  1.7 0.9 %copy-done.1 = f32[256,256]{1,0:T(8,128)S(1)} copy-done((f32[256,256]{1,0:T(8,128)S(1)}, f32[256,256]{1,0:T(8,128)}, u32[]{:S(2)}) %copy-start.1) | copy-done | bytes 262168
  2.6 0.0 copy-start.2
  2.6 0.8 %copy-done.2 = f32[64,256]{1,0:T(8,128)S(1)} copy-done((f32[64,256]{1,0:T(8,128)S(1)}, f32[64,256]{1,0:T(8,128)}, u32[]{:S(2)}) %copy-start.2) | copy-done | bytes 65560
  3.5 42.7 %shard_map.50 = (f32[512,256]{1,0:T(8,128)S(1)}, f32[64,256]{1,0:T(8,128)S(1)}) custom-call(f32[512,256]{1,0:T(8,128)S(1)} %copy-done, f32[64,256]{1,0:T(8,128)S(1)} %copy-done.2, f32[256,256]{1,0:T(8,128)S(1)} %copy-done.1), custom_call_target="tpu_custom_call" | custom-call | tf_op jit(solution)/shard_map/pallas_call | solution.py:283
  46.2 0.8 %shard_map.51 = (f32[512,256]{1,0:T(8,128)}, f32[64,256]{1,0:T(8,128)}) custom-call(f32[512,256]{1,0:T(8,128)S(1)} %get-tuple-element.4.held_ref, f32[64,256]{1,0:T(8,128)S(1)} %get-tuple-element.5.held_corr_ref), custom_call_target="tpu_custom_call" | custom-call | tf_op jit(solution)/shard_map/pallas_call | solution.py:311
Async XLA Ops:
  0.6 1.0 %copy-start = (f32[512,256]{1,0:T(8,128)S(1)}, f32[512,256]{1,0:T(8,128)}, u32[]{:S(2)}) copy-start(f32[512,256]{1,0:T(8,128)} %a_ref.1) | copy-start | bytes 1572868
  1.7 0.9 %copy-start.1 = (f32[256,256]{1,0:T(8,128)S(1)}, f32[256,256]{1,0:T(8,128)}, u32[]{:S(2)}) copy-start(f32[256,256]{1,0:T(8,128)} %t_ref.1) | copy-start | bytes 786436
  2.6 0.8 %copy-start.2 = (f32[64,256]{1,0:T(8,128)S(1)}, f32[64,256]{1,0:T(8,128)}, u32[]{:S(2)}) copy-start(f32[64,256]{1,0:T(8,128)} %panel_ref.1) | copy-start | bytes 196612
